TPU v7x, 128 devices: a whole 4x4x4 slice. The times are simulated.
128 devices in a mesh: row: 16 (over y_hi, x, core), loop: 8 (over z, y_lo).
Axes of the slice: x: 4, y: 4 (y_hi: 2, y_lo: 2; y = y_hi * 2 + y_lo), z: 4, core: 2. Of those that a mesh axis runs over, the one named last changes fastest.
Arguments:
- features: bfloat16 [262144, 256], P(('row', 'loop')), may hold values from -6 to 6
- weight: bfloat16 [256, 256], replicated, may hold values from -0.375 to 0.375
- local_tiles: bfloat16 [16384, 128, 128], P(('row', 'loop')), may hold values from -0.1875 to 0.1875
- local_ids: int32 [16384], P(('row', 'loop')), may hold values from 0 to 255, as said below
- local_live: int32 [16384], P(('row', 'loop')), may hold values 0 or 1
- send_rows: int32 [128, 16, 256], P(('row', 'loop')), may hold values from 0 to 2047
- send_count: int32 [128, 16], P(('row', 'loop')), may hold values from 0 to 256, as said below
- edge_tiles: bfloat16 [36864, 128, 128], P(('row', 'loop')), may hold values from -0.1875 to 0.1875
- edge_ids: int32 [36864], P(('row', 'loop')), may hold values from 0 to 511, as said below
- edge_live: int32 [36864], P(('row', 'loop')), may hold values 0 or 1
- hub_feats: bfloat16 [2048, 256], P('loop'), may hold values from -6 to 6
- hub_adj: bfloat16 [262144, 2048], P(('row', 'loop')), may hold values from -0.1875 to 0.1875
- hub_live: int32 [2048, 16], P(('row', 'loop')), may hold values 0 or 1
Outputs:
- layer_out: bfloat16 [262144, 256], P(('row', 'loop'))
Inputs may be any that keep to these rules, and one draw needn't show every extreme that they name: `local_ids`: each entry is i * 16 + j, a tile of one block's 16 x 16 grid; the 128 entries of one device are distinct. `edge_ids`: each entry is i * 32 + j, a tile of a 16 x 32 grid; the 288 entries of one device are distinct. Only the first send_count[d, s] slots of send_rows[d, s] are sent with data. For every loop index, all devices of that loop index send 256 rows to one common row index.
All inputs are finite; a program needn't handle non-finite values. No bound on the sum of `local_live` or of `edge_live` or of `hub_live` on one device may be relied on, other than what follows from the above.
Results may differ from a plain program's by a relative error of at most 0.005.
Values may be sent and summed in bfloat16 or wider, within the bound.
A program may use at most 256 MiB of HBM per device.

v0:
```python
import jax
import jax.numpy as jnp
from jax import lax
from jax.sharding import PartitionSpec as P


def tile_term(tile_set, tile_ids, tile_live, panels, out_tiles, in_tiles):
    tile_size = tile_set.shape[1]
    width = panels.shape[1]
    live_float = tile_live.astype(jnp.float32)
    panel_grid = panels.reshape(in_tiles, tile_size * width)
    col_select = ((tile_ids % in_tiles)[:, None] == jnp.arange(in_tiles)[None, :]).astype(
        jnp.bfloat16
    )
    gathered = jnp.dot(col_select, panel_grid, preferred_element_type=jnp.float32).astype(
        jnp.bfloat16
    )
    gathered = gathered.reshape(tile_ids.shape[0], tile_size, width)
    products = jnp.einsum("tab,tbf->taf", tile_set, gathered, preferred_element_type=jnp.float32)
    row_select = ((tile_ids // in_tiles)[None, :] == jnp.arange(out_tiles)[:, None]).astype(
        jnp.float32
    )
    row_select = row_select * live_float[None, :]
    summed = jnp.dot(
        row_select,
        products.reshape(tile_ids.shape[0], tile_size * width),
        precision=lax.Precision.HIGHEST,
    )
    return summed.reshape(out_tiles * tile_size, width)


def per_device(
    features,
    weight,
    local_tiles,
    local_ids,
    local_live,
    send_rows,
    send_count,
    edge_tiles,
    edge_ids,
    edge_live,
    hub_feats,
    hub_adj,
    hub_live,
):
    row_count, width = features.shape
    tile_size = local_tiles.shape[1]
    row_tiles = row_count // tile_size
    peers = lax.axis_size("row")
    slot_count = send_rows.shape[2]
    picked = features[send_rows[0]]
    kept_mask = jnp.arange(slot_count)[None, :] < send_count[0][:, None]
    outgoing = jnp.where(kept_mask[:, :, None], picked, jnp.zeros((), jnp.bfloat16))
    incoming = lax.all_to_all(outgoing, "row", split_axis=0, concat_axis=0, tiled=True)
    received = incoming.reshape(peers * slot_count, width)
    local_sum = tile_term(local_tiles, local_ids, local_live, features, row_tiles, row_tiles)
    edge_sum = tile_term(
        edge_tiles, edge_ids, edge_live, received, row_tiles, peers * slot_count // tile_size
    )
    hub_mask = jnp.repeat(jnp.repeat(hub_live, tile_size, 0), tile_size, 1).astype(jnp.bfloat16)
    masked_adj = hub_adj * hub_mask
    hub_sum = jnp.dot(
        masked_adj,
        lax.all_gather(hub_feats, "loop", axis=0, tiled=True),
        preferred_element_type=jnp.float32,
    )
    aggregated = (local_sum + edge_sum + hub_sum).astype(jnp.bfloat16)
    return jax.nn.relu(jnp.dot(aggregated, weight, preferred_element_type=jnp.float32)).astype(
        jnp.bfloat16
    )


def solution(mesh):
    placed = (
        P(("row", "loop"), None),
        P(),
        P(("row", "loop"), None, None),
        P(("row", "loop")),
        P(("row", "loop")),
        P(("row", "loop"), None, None),
        P(("row", "loop"), None),
        P(("row", "loop"), None, None),
        P(("row", "loop")),
        P(("row", "loop")),
        P("loop", None),
        P(("row", "loop"), None),
        P(("row", "loop"), None),
    )
    return jax.shard_map(
        per_device, mesh=mesh, in_specs=placed, out_specs=P(("row", "loop"), None), check_vma=False
    )
```

profile of v0, /device:TPU:1, one launch (start us, length us, event | category | flops | bytes accessed | tf_op | source)
XLA Modules:
  0.0 242.4 jit_solution(10806304572988081894)
XLA Ops:
  6.5 0.0 copy-start
  6.5 0.8 fusion.8
  7.3 0.7 iota_compare_fusion.6
  8.1 14.3 %gather_fusion = bf16[4096,256]{1,0:T(8,128)(2,1)S(1)} fusion(bf16[2048,256]{1,0:T(8,128)(2,1)} %param.13, s32[4096]{0:T(1024)S(1)} %broadcast_clamp_fusion), kind=kCustom, calls=%fused_computation | custom fusion | bytes 4210688 | tf_op jit(solution)/shard_map/gather | solution.py:52
  22.4 0.0 copy-start.1
  22.4 0.0 copy-start.6
  22.4 1.7 broadcast_select_fusion
  24.2 8.4 %all-to-all-start = ((bf16[16,256,256]{2,1,0:T(8,128)(2,1)}), bf16[16,256,256]{2,1,0:T(8,128)(2,1)}, u32[]{:S(2)}, u32[]{:S(2)}) async-start(bf16[16,256,256]{2,1,0:T(8,128)(2,1)} %broadcast_select_fusion), calls=%async_computation | async-start | bytes 4194304 | tf_op jit(solution)/shard_map/all_to_all | solution.py:55
  32.6 0.0 all-gather.2.cloned.1.call-start
  32.7 0.7 all-gather.2.cloned.1.call-update
  33.4 0.0 copy-done.1
  33.4 0.5 reshape.80
  33.9 5.6 %convolution_convert_fusion.1 = bf16[128,32768]{1,0:T(8,128)(2,1)} fusion(bf16[16,32768]{1,0:T(8,128)(2,1)S(1)} %reshape.80, s32[128]{0:T(128)S(1)} %get-tuple-element.8), kind=kOutput, calls=%fused_computation.2 | convolution fusion | flops 138414080 | bytes 9437696 | tf_op jit(solution)/shard_map/dot_general | solution.py:15
  39.5 9.1 %copy.22 = bf16[16,8,128,256]{3,2,1,0:T(8,128)(2,1)} copy(bf16[16,8,128,256]{3,1,2,0:T(8,128)(2,1)} %bitcast.47) | data formatting | bytes 16777216
  48.6 12.7 %convolution_bitcast_fusion.1 = f32[128,128,256]{1,2,0:T(8,128)} fusion(bf16[128,128,256]{2,1,0:T(8,128)(2,1)} %bitcast.46, bf16[128,128,128]{2,1,0:T(8,128)(2,1)} %param.15), kind=kOutput, calls=%fused_computation.5 | convolution fusion | flops 1073741824 | bytes 29360128 | tf_op jit(solution)/shard_map/tab,tbf->taf/dot_general | solution.py:19
  61.3 17.7 %copy.17 = f32[128,128,256]{0,2,1:T(8,128)} copy(f32[128,128,256]{1,2,0:T(8,128)} %convolution_bitcast_fusion.1) | data formatting | bytes 33554432 | tf_op jit(solution)/shard_map/tab,tbf->taf/dot_general | solution.py:19
  79.0 0.0 copy-done.7
  79.1 0.0 copy-done.2
  79.1 0.0 copy-done.3
  79.1 16.6 %fusion.12 = f32[16,32768]{1,0:T(8,128)S(1)} fusion(f32[128,32768]{0,1:T(8,128)} %bitcast.45, f32[128]{0:T(128)S(1)} %convert_element_type.33, s32[128]{0:T(128)S(1)} %get-tuple-element.7), kind=kOutput, calls=%fused_computation.27 | convolution fusion | flops 805310464 | bytes 18875392 | tf_op jit(solution)/shard_map/dot_general | solution.py:24
  95.7 0.0 all-to-all-done
  95.7 4.2 %reshape_reshape.3 = bf16[32,32768]{1,0:T(8,128)(2,1)} reshape(bf16[16,256,256]{2,1,0:T(8,128)(2,1)} %all-to-all-done) | data formatting | bytes 4194304 | tf_op jit(solution)/shard_map/reshape;reshape | solution.py:11
  99.9 10.7 %convolution_convert_fusion = bf16[288,32768]{1,0:T(8,128)(2,1)} fusion(bf16[32,32768]{1,0:T(8,128)(2,1)} %reshape_reshape.3, s32[288]{0:T(512)S(1)} %get-tuple-element.6), kind=kOutput, calls=%fused_computation.1 | convolution fusion | flops 613426176 | bytes 20972672 | tf_op jit(solution)/shard_map/dot_general | solution.py:15
  110.6 18.4 %copy.24 = bf16[36,8,128,256]{3,2,1,0:T(8,128)(2,1)} copy(bf16[36,8,128,256]{3,1,2,0:T(8,128)(2,1)} %bitcast.43) | data formatting | bytes 37748736
  129.0 22.4 %convolution_bitcast_fusion = f32[288,128,256]{1,2,0:T(8,128)} fusion(bf16[288,128,256]{2,1,0:T(8,128)(2,1)} %bitcast.44, bf16[288,128,128]{2,1,0:T(8,128)(2,1)} %param.20), kind=kOutput, calls=%fused_computation.4 | convolution fusion | flops 2415919104 | bytes 66060288 | tf_op jit(solution)/shard_map/tab,tbf->taf/dot_general | solution.py:19
  151.4 36.9 %copy.25 = f32[36,8,128,256]{3,1,2,0:T(8,128)} copy(f32[36,8,128,256]{2,3,1,0:T(8,128)} %bitcast.42) | data formatting | bytes 75497472
  188.3 25.7 %convolution_add_fusion = f32[16,32768]{1,0:T(8,128)} fusion(f32[16,32768]{1,0:T(8,128)S(1)} %fusion.12, f32[288,32768]{1,0:T(8,128)} %bitcast.41, f32[288]{0:T(512)S(1)} %convert_element_type.35, s32[288]{0:T(512)S(1)} %get-tuple-element.5), kind=kOutput, calls=%fused_computation.3 | convolution fusion | flops 1812472832 | bytes 41945344 | tf_op jit(solution)/shard_map/dot_general | solution.py:24
  214.0 1.7 add.41
  215.7 0.0 all-gather.2.cloned.1.call-done
  215.8 0.1 broadcast_in_dim.18
  215.8 9.9 %broadcast_in_dim.19 = bf16[2048,16,128]{2,1,0:T(8,128)(2,1)} broadcast(bf16[2048,16]{1,0:T(8,128)(2,1)S(1)} %bitcast.50), dimensions={0,1} | broadcast | bytes 8454144 | tf_op jit(solution)/shard_map/broadcast_in_dim | solution.py:61
  225.8 9.8 %fusion.4 = bf16[2048,256]{1,0:T(8,128)(2,1)} fusion(bf16[256,256]{1,0:T(8,128)(2,1)S(1)} %copy-done, f32[2048,256]{1,0:T(8,128)S(1)} %add.41, bf16[2048,256]{1,0:T(8,128)(2,1)S(1)} %copy-done.5, bf16[2048,2048]{1,0:T(8,128)(2,1)} %param.24, bf16[256,8,16,128]{3,2,1,0:T(8,128)(2,1)} %bitcast.48), kind=kOutput, calls=%fused_computation.12 | convolution fusion | flops 2422210560 | bytes 21102592 | tf_op jit(solution)/shard_map/dot_general | solution.py:69
  (16 shorter events, 0.1 us)
Async XLA Ops:
  6.5 219.3 %copy-start = (bf16[256,256]{1,0:T(8,128)(2,1)S(1)}, bf16[256,256]{1,0:T(8,128)(2,1)}, u32[]{:S(2)}) copy-start(bf16[256,256]{1,0:T(8,128)(2,1)} %param.14) | copy-start | bytes 393220
  22.4 11.0 %copy-start.1 = (bf16[2048,256]{1,0:T(8,128)(2,1)S(1)}, bf16[2048,256]{1,0:T(8,128)(2,1)}, u32[]{:S(2)}) copy-start(bf16[2048,256]{1,0:T(8,128)(2,1)} %param.13) | copy-start | bytes 3145732
  22.4 11.5 %copy-start.6 = (s32[128]{0:T(128)S(1)}, s32[128]{0:T(128)}, u32[]{:S(2)}) copy-start(s32[128]{0:T(128)} %param.16) | copy-start | bytes 1540
  24.2 71.5 %all-to-all-start = ((bf16[16,256,256]{2,1,0:T(8,128)(2,1)}), bf16[16,256,256]{2,1,0:T(8,128)(2,1)}, u32[]{:S(2)}, u32[]{:S(2)}) async-start(bf16[16,256,256]{2,1,0:T(8,128)(2,1)} %broadcast_select_fusion), calls=%async_computation | async-start | bytes 4194304 | tf_op jit(solution)/shard_map/all_to_all | solution.py:55
  32.6 183.1 %all-gather.2.cloned.1.call-start = ((), (), s32[]{:S(2)}) async-start(), calls=%async_computation.1 | async-start | bytes 1179648 | tf_op jit(solution)/shard_map/all_gather | solution.py:65
  61.3 17.7 %copy-start.7 = (s32[128]{0:T(128)S(1)}, s32[128]{0:T(128)}, u32[]{:S(2)}) copy-start(s32[128]{0:T(128)} %param.17) | copy-start | bytes 1540
  61.3 17.7 %copy-start.4 = (s32[288]{0:T(512)S(1)}, s32[288]{0:T(512)}, u32[]{:S(2)}) copy-start(s32[288]{0:T(512)} %param.22) | copy-start | bytes 3460
  61.3 17.7 %copy-start.2 = (s32[16,16]{1,0:T(8,128)S(1)}, s32[16,16]{1,0:T(8,128)}, u32[]{:S(2)}) copy-start(s32[16,16]{1,0:T(8,128)} %param.25) | copy-start | bytes 3076
  61.3 17.7 %copy-start.3 = (s32[288]{0:T(512)S(1)}, s32[288]{0:T(512)}, u32[]{:S(2)}) copy-start(s32[288]{0:T(512)} %param.21) | copy-start | bytes 3460
  215.8 10.0 %copy-start.5 = (bf16[2048,256]{1,0:T(8,128)(2,1)S(1)}, bf16[2048,256]{1,0:T(8,128)(2,1)}, u32[]{:S(2)}) copy-start(bf16[2048,256]{1,0:T(8,128)(2,1)} %all-gather.2.cloned.1.call-done) | copy-start | bytes 3145732
Sparse Core Ops, SparseCore 0:
  35.1 48.2 all-gather.1
where the time goes:
time: 244 us; the launch traced here: 242 us
  local copies, waits for them, and re-layouts  113 us (46%)
  matrix products  104 us (43%)
  between operations  13.6 us (6%)
  starting transfers between devices  8.48 us (3%)
  other arithmetic  3.27 us (1%)
    unnamed x20, local copies, waits for them, and re-layouts  64.4 us
    dot_general x2, matrix products, tile_term(): jnp.dot(row_select, products.reshape(tile_ids.shape[0], tile_size * width...  42.3 us
    dot_general x2, matrix products, tile_term(): jnp.einsum('tab,tbf->taf', tile_set, gathered, preferred_element_type=jnp...  35.1 us
    dot_general x1, local copies, waits for them, and re-layouts, tile_term(): jnp.einsum('tab,tbf->taf', tile_set, gathered, preferred_element_type=jnp...  17.7 us
    dot_general x2, matrix products, tile_term(): jnp.dot(col_select, panel_grid, preferred_element_type=jnp.float32)  16.3 us
    gather x1, local copies, waits for them, and re-layouts, per_device(): picked = features[send_rows[0]]  14.3 us
    broadcast_in_dim x1, local copies, waits for them, and re-layouts, per_device(): jnp.repeat(jnp.repeat(hub_live, tile_size, 0), tile_size, 1)  9.95 us
    dot_general x1, matrix products, per_device(): jnp.dot(aggregated, weight, preferred_element_type=jnp.float32)  9.8 us
  transfers between devices with their start and end apart: 2, of which 0 were waited for; matrix products, arithmetic and copies ran while one was open for 75% of the time, Pallas kernels for 0%

commit v1 on v0

v1 whole, which is shorter than its diff:
```python
import functools

import jax
import jax.numpy as jnp
from jax import lax
from jax.experimental import pallas as pl
from jax.experimental.pallas import tpu as pltpu
from jax.sharding import PartitionSpec as P

MESH = pl.DeviceIdType.MESH
BF16 = jnp.bfloat16
F32 = jnp.float32
I32 = jnp.int32
TILE = 128
PIECE = 64
OWN = 12


def offset(k):
    return 1 - k // 8, (2 + 3 * ((k // 2) % 4)) % 4, k % 2


def partner(r, k, sign):
    dy, dx, dc = offset(k)
    y, x, c = r // 8, (r // 2) % 4, r % 2
    return ((y + dy) % 2) * 8 + ((x + sign * dx + 4) % 4) * 2 + (c + dc) % 2


def dot(a, b):
    return jnp.dot(a, b, preferred_element_type=F32)


def slot_table(edge_ids, edge_live, local_ids, local_live, hub_live):
    nedge, nloc, nrow = edge_ids.shape[0], local_ids.shape[0], hub_live.shape[0]
    ids = jnp.concatenate([edge_ids, local_ids + 512])
    live = jnp.concatenate([edge_live, local_live]) > 0
    slot = jnp.concatenate([jnp.arange(nedge) - nedge, jnp.arange(nloc) - nloc]).astype(I32)
    hit = jnp.logical_and(ids[:, None] == jnp.arange(768)[None, :], live[:, None])
    least = jnp.min(jnp.where(hit, slot[:, None], 0), axis=0)
    table = least + jnp.where(jnp.arange(768) < 512, nedge, nloc)
    hub = jnp.where(hub_live == 0, nrow, jnp.arange(nrow)[:, None])
    return jnp.concatenate([table, hub.reshape(-1)]).astype(I32)


def kernel(
    send_rows,
    tabs,
    send_count,
    features,
    weight,
    local_tiles,
    edge_tiles,
    hub_feats,
    hub_adj,
    out,
    feats,
    wts,
    loc,
    edg,
    hraw,
    hubf,
    a1,
    a2,
    send,
    recv,
    acc,
    outv,
    oh,
    rowsk,
    colk,
    in_sem,
    out_sem,
    ssem,
    rsem,
    hs_sem,
    hr_sem,
):
    r = lax.axis_index("row")
    l = lax.axis_index("loop")
    core = r % 2
    z, ylo = l // 2, l % 2
    sib = r + 1 - 2 * core
    nloc = local_tiles.shape[0]
    nedge = edge_tiles.shape[0]
    nrow = hub_adj.shape[0]

    def load(src, dst, n):
        return pltpu.make_async_copy(src, dst, in_sem.at[n])

    c_feat = load(features, feats, 0)
    c_feat.start()
    c_hub = load(hub_feats.at[pl.ds(core * TILE, TILE)], hubf.at[core, l], 1)
    c_hub.start()
    c_w = load(weight, wts, 2)
    c_w.start()
    c_loc = load(local_tiles, loc.at[pl.ds(0, nloc)], 3)
    c_loc.start()
    c_adj = load(hub_adj, hraw.at[pl.ds(0, nrow)], 4)
    c_adj.start()
    c_edge = load(edge_tiles, edg.at[pl.ds(0, nedge)], 5)
    c_edge.start()

    barrier = pltpu.get_barrier_semaphore()

    def greet(device):
        pl.semaphore_signal(barrier, inc=1, device_id=device, device_id_type=MESH)

    @pl.loop(0, 15)
    def _(n):
        greet({"row": (r + 1 + n) % 16, "loop": l})

    greet({"row": r, "loop": z * 2 + 1 - ylo})
    for dz in (1, 2, 3):
        greet({"row": r, "loop": ((z + dz) % 4) * 2 + ylo})

    rowsk[...] = jnp.full(rowsk.shape, -1, I32)
    slot = lax.broadcasted_iota(I32, (1, 4 * PIECE), 1)
    for k in range(16):
        s = partner(r, k, 1)
        row = send_rows[pl.ds(s, 1), :]
        rowsk[pl.ds(k, 1), :] = jnp.where(slot < send_count[0, s], row, -1)
    colk[...] = jnp.transpose(rowsk[...])

    loc[nloc] = jnp.zeros((TILE, TILE), BF16)
    edg[nedge] = jnp.zeros((TILE, TILE), BF16)
    hraw[nrow] = jnp.zeros((TILE, hraw.shape[2]), BF16)

    c_feat.wait()
    c_hub.wait()
    pl.semaphore_wait(barrier, 19)

    def remote(src, dst, s1, s2, device):
        return pltpu.make_async_remote_copy(
            src_ref=src, dst_ref=dst, send_sem=s1, recv_sem=s2, device_id=device, device_id_type=MESH
        )

    def piece(k, p, sign=1):
        return remote(
            send.at[k, pl.ds(p * PIECE, PIECE)],
            recv.at[p // 2, pl.ds(k * TILE + (p % 2) * PIECE, PIECE)],
            ssem.at[p, k],
            rsem.at[p, k],
            {"row": partner(r, k, 1), "loop": l},
        )

    def hub_step(n, lsrc, device):
        return remote(hubf.at[core, lsrc], hubf.at[core, lsrc], hs_sem.at[n], hr_sem.at[n], device)

    def hub_in(n, lsrc, half):
        return remote(
            hubf.at[half, lsrc], hubf.at[half, lsrc], hs_sem.at[n], hr_sem.at[n], {"row": sib, "loop": l}
        )

    l_y = z * 2 + 1 - ylo

    def zpeer(dz, own):
        return ((z + dz) % 4) * 2 + (ylo if own else 1 - ylo)

    hub_y = hub_step(0, l, {"row": r, "loop": l_y})
    hub_y.start()
    hub_z = [hub_step(dz, l, {"row": r, "loop": zpeer(dz, True)}) for dz in (1, 2, 3)]
    for c in hub_z:
        c.start()

    lane = lax.broadcasted_iota(I32, (4 * PIECE, TILE), 1)

    @pl.loop(0, 4)
    def _(p):
        cols = colk[pl.ds(pl.multiple_of(p * PIECE, PIECE), PIECE), :]
        for a in range(4):
            idx = jnp.concatenate(
                [jnp.broadcast_to(cols[:, k : k + 1], (PIECE, TILE)) for k in range(4 * a, 4 * a + 4)], 0
            )
            for c in range(feats.shape[0] // TILE):
                oh[:, c * TILE : (c + 1) * TILE] = jnp.where(idx == lane + c * TILE, 1.0, 0.0).astype(BF16)
            picked = dot(oh[...], feats[...]).astype(BF16)
            for d in range(4):
                k = 4 * a + d
                part = picked[d * PIECE : (d + 1) * PIECE]
                if k == OWN:
                    recv[p // 2, pl.ds(pl.multiple_of(k * TILE + (p % 2) * PIECE, PIECE), PIECE), :] = part
                else:
                    send[k, pl.ds(pl.multiple_of(p * PIECE, PIECE), PIECE), :] = part
                    piece(k, p).start()

    hub_in(0, l_y, core).wait_recv()
    hub_f = [hub_step(3 + dz, l_y, {"row": r, "loop": zpeer(dz, True)}) for dz in (1, 2, 3)]
    for c in hub_f:
        c.start()

    nm = 4
    mb = acc.shape[0] // nm

    def rows_of(m):
        return pl.ds(pl.multiple_of(m * mb, mb), mb)

    c_loc.wait()

    @pl.loop(0, 16)
    def _(i):
        at = pl.ds(pl.multiple_of(i * TILE, TILE), TILE)
        for j in range(16):
            a1[at, j * TILE : (j + 1) * TILE] = loc[tabs[512 + 16 * i + j]]

    @pl.loop(0, nm)
    def _(m):
        acc[rows_of(m), :] = dot(a1[rows_of(m), :], feats[...])

    for dz in (1, 2, 3):
        hub_in(dz, ((z + 4 - dz) % 4) * 2 + ylo, core).wait_recv()
        hub_in(3 + dz, ((z + 4 - dz) % 4) * 2 + 1 - ylo, core).wait_recv()
    hub_c = remote(hubf.at[core], hubf.at[core], hs_sem.at[7], hr_sem.at[7], {"row": sib, "loop": l})
    hub_c.start()

    c_adj.wait()

    @pl.loop(0, 16)
    def _(i):
        at = pl.ds(pl.multiple_of(i * TILE, TILE), TILE)
        for b in range(16):
            n = (b % 2) * 8 + b // 2
            a2[at, n * TILE : (n + 1) * TILE] = hraw[tabs[768 + 16 * i + b], :, b * TILE : (b + 1) * TILE]

    remote(hubf.at[1 - core], hubf.at[1 - core], hs_sem.at[7], hr_sem.at[7], {"row": sib, "loop": l}).wait_recv()

    @pl.loop(0, nm)
    def _(m):
        hub_all = hubf[...].reshape(16 * TILE, hubf.shape[3])
        acc[rows_of(m), :] += dot(a2[rows_of(m), :], hub_all)

    c_edge.wait()

    def lay_edges(h, a):
        @pl.loop(0, 16)
        def _(i):
            at = pl.ds(pl.multiple_of(i * TILE, TILE), TILE)
            for k in range(16):
                a[at, k * TILE : (k + 1) * TILE] = edg[tabs[32 * i + 2 * partner(r, k, -1) + h]]

    lay_edges(0, a1)
    lay_edges(1, a2)
    for p in (0, 1):
        for k in range(16):
            if k != OWN:
                piece(k, p).wait_recv()

    @pl.loop(0, nm)
    def _(m):
        acc[rows_of(m), :] += dot(a1[rows_of(m), :], recv[0])

    group = 4
    for g in range(4):
        span = slice(g * group * TILE, (g + 1) * group * TILE)
        for p in (2, 3):
            for k in range(g * group, (g + 1) * group):
                if k != OWN:
                    piece(k, p).wait_recv()
        if g < 3:

            @pl.loop(0, nm)
            def _(m):
                acc[rows_of(m), :] += dot(a2[rows_of(m), span], recv[1, span, :])

    c_w.wait()

    @pl.loop(0, nm)
    def _(m):
        at = rows_of(m)
        agg = (acc[at, :] + dot(a2[at, span], recv[1, span, :])).astype(BF16)
        outv[at, :] = jnp.maximum(dot(agg, wts[...]), 0.0).astype(BF16)
        pltpu.make_async_copy(outv.at[at], out.at[at], out_sem.at[m]).start()

    hub_y.wait_send()
    for c in hub_z + hub_f:
        c.wait_send()
    hub_c.wait_send()

    @pl.loop(0, 4)
    def _(p):
        for k in range(16):
            if k != OWN:
                piece(k, p).wait_send()

    @pl.loop(0, nm)
    def _(m):
        at = rows_of(m)
        pltpu.make_async_copy(outv.at[at], out.at[at], out_sem.at[m]).wait()


def per_device(
    features,
    weight,
    local_tiles,
    local_ids,
    local_live,
    send_rows,
    send_count,
    edge_tiles,
    edge_ids,
    edge_live,
    hub_feats,
    hub_adj,
    hub_live,
):
    rows, width = features.shape
    nloc, nedge = local_tiles.shape[0], edge_tiles.shape[0]
    tabs = slot_table(edge_ids, edge_live, local_ids, local_live, hub_live)
    vmem = pl.BlockSpec(memory_space=pltpu.VMEM)
    smem = pl.BlockSpec(memory_space=pltpu.SMEM)
    hbm = pl.BlockSpec(memory_space=pl.ANY)
    dma = pltpu.SemaphoreType.DMA
    return pl.pallas_call(
        kernel,
        out_shape=jax.ShapeDtypeStruct((rows, width), BF16),
        in_specs=[vmem, smem, smem, hbm, hbm, hbm, hbm, hbm, hbm],
        out_specs=hbm,
        scratch_shapes=[
            pltpu.VMEM((rows, width), BF16),
            pltpu.VMEM((width, width), BF16),
            pltpu.VMEM((nloc + 1, TILE, TILE), BF16),
            pltpu.VMEM((nedge + 1, TILE, TILE), BF16),
            pltpu.VMEM((rows // TILE + 1, TILE, 16 * TILE), BF16),
            pltpu.VMEM((2, 8, TILE, width), BF16),
            pltpu.VMEM((rows, 16 * TILE), BF16),
            pltpu.VMEM((rows, 16 * TILE), BF16),
            pltpu.VMEM((16, 4 * PIECE, width), BF16),
            pltpu.VMEM((2, 16 * TILE, width), BF16),
            pltpu.VMEM((rows, width), F32),
            pltpu.VMEM((rows, width), BF16),
            pltpu.VMEM((4 * PIECE, rows), BF16),
            pltpu.VMEM((TILE, 4 * PIECE), I32),
            pltpu.VMEM((4 * PIECE, TILE), I32),
            dma((6,)),
            dma((4,)),
            dma((4, 16)),
            dma((4, 16)),
            dma((8,)),
            dma((8,)),
        ],
        compiler_params=pltpu.CompilerParams(
            collective_id=0, has_side_effects=True, vmem_limit_bytes=58 * 1024 * 1024
        ),
        cost_estimate=pl.CostEstimate(flops=13 * 10**9, bytes_accessed=24 * 2**20, transcendentals=0),
    )(
        send_rows[0],
        tabs,
        send_count,
        features,
        weight,
        local_tiles,
        edge_tiles,
        hub_feats,
        hub_adj.reshape(rows // TILE, TILE, hub_adj.shape[1]),
    )


def solution(mesh):
    both = ("row", "loop")
    placed = (
        P(both, None),
        P(),
        P(both, None, None),
        P(both),
        P(both),
        P(both, None, None),
        P(both, None),
        P(both, None, None),
        P(both),
        P(both),
        P("loop", None),
        P(both, None),
        P(both, None),
    )
    return jax.shard_map(per_device, mesh=mesh, in_specs=placed, out_specs=P(both, None), check_vma=False)
```

time: 244 us -> 53.4 us (0.22)
  local copies, waits for them, and re-layouts: 113 us -> 2.34 us
  matrix products: 104 us -> 0 us
  Pallas kernels: 0 us -> 46.8 us
  between operations: 13.6 us -> 0.03 us
  starting transfers between devices: 8.48 us -> 0 us
    dot_general x7 -> x0, matrix products: 104 us -> none  [the longest x2 42.3 us: tile_term(): jnp.dot(row_select, products.reshape(tile_ids.shape[0], tile_size * width...]
    unnamed x20 -> x1, local copies, waits for them, and re-layouts: 64.4 us -> 2.26 us
    pallas_call x0 -> x1, Pallas kernels: none -> 46.8 us  [per_device(): pl.pallas_call(kernel, out_shape=jax.ShapeDtypeStruct((rows, width), BF16...]
    dot_general x1 -> x0, local copies, waits for them, and re-layouts: 17.7 us -> none  [tile_term(): jnp.einsum('tab,tbf->taf', tile_set, gathered, preferred_element_type=jnp...]
    gather x1 -> x0, local copies, waits for them, and re-layouts: 14.3 us -> none  [per_device(): picked = features[send_rows[0]]]
    broadcast_in_dim x2 -> x0, local copies, waits for them, and re-layouts: 10 us -> none  [the longest x1 9.95 us: per_device(): jnp.repeat(jnp.repeat(hub_live, tile_size, 0), tile_size, 1)]
    all_to_all x1 -> x0, starting transfers between devices: 8.45 us -> none  [per_device(): lax.all_to_all(outgoing, 'row', split_axis=0, concat_axis=0, tiled=True)]
    another operation x1 -> x0, local copies, waits for them, and re-layouts: 4.19 us -> none  [tile_term(): panel_grid = panels.reshape(in_tiles, tile_size * width)]
  transfers between devices with their start and end apart: 2 -> 0, of which waited for: 0 -> 0; matrix products, arithmetic and copies ran while one was open for 75% -> 0% of each run, Pallas kernels for 0% -> 0%
where the time goes in v1:
time: 53.4 us; the launch traced here: 53.1 us
  Pallas kernels  46.8 us (88%)
  other arithmetic  3.9 us (7%)
  local copies, waits for them, and re-layouts  2.34 us (4%)
    pallas_call x1, Pallas kernels, per_device(): pl.pallas_call(kernel, out_shape=jax.ShapeDtypeStruct((rows, width), BF16...  46.8 us
    unnamed x1, local copies, waits for them, and re-layouts  2.26 us

profile of v1, /device:TPU:1, one launch (start us, length us, event | category | flops | bytes accessed | tf_op | source)
XLA Modules:
  0.0 53.1 jit_solution(12898435552456212948)
XLA Ops:
  0.0 0.7 %broadcast_add_fusion = s32[128]{0:T(128)S(1)} fusion(s32[128]{0:T(128)} %param.16), kind=kLoop, calls=%fused_computation.12 | loop fusion | flops 128 | bytes 1024 | tf_op jit(solution)/shard_map/add | solution.py:35
  0.7 0.8 %add_compare_fusion = pred[416]{0:T(512)(128)(4,1)S(1)} fusion(s32[128]{0:T(128)} %param.17, s32[288]{0:T(512)} %param.22), kind=kLoop, calls=%fused_computation.8 | loop fusion | flops 832 | bytes 2080 | tf_op jit(solution)/shard_map/gt | solution.py:36
  1.4 0.8 %pad_add_fusion.1 = (s32[416]{0:T(512)S(1)}, s32[416]{0:T(512)S(1)}) fusion(s32[128]{0:T(128)S(1)} %broadcast_add_fusion, s32[288]{0:T(512)} %param.21, s32[128]{0:T(128)S(1)} %iota_add_fusion.1, s32[288]{0:T(512)S(1)} %iota_add_fusion), kind=kLoop, calls=%fused_computation.7 | loop fusion | flops 832 | bytes 6656 | tf_op jit(solution)/shard_map/concatenate | solution.py:35
  2.2 0.4 select_reduce_fusion
  2.6 0.7 %iota_select_fusion = s32[16,16]{1,0:T(8,128)S(1)} fusion(s32[16,16]{1,0:T(8,128)} %param.25), kind=kLoop, calls=%fused_computation.3 | loop fusion | flops 512 | bytes 2048 | tf_op jit(solution)/shard_map/jit(_where)/select_n | solution.py:41
  3.3 0.1 reshape.23
  3.4 0.6 %pad_add_fusion.tabs = s32[1024]{0:T(1024)} fusion(s32[256]{0:T(256)S(1)} %reshape.23, s32[768]{0:T(1024)S(1)} %select_add_fusion), kind=kLoop, calls=%fused_computation.4 | loop fusion | flops 1024 | bytes 8192 | tf_op jit(solution)/shard_map/concatenate | solution.py:42
  4.0 46.8 %shard_map.127 = bf16[2048,256]{1,0:T(8,128)(2,1)} custom-call(s32[16,256]{1,0:T(8,128)} %bitcast.3, s32[1024]{0:T(1024)} %pad_add_fusion.tabs, s32[1,16]{1,0:T(1,128)} %send_count.1, bf16[2048,256]{1,0:T(8,128)(2,1)} %features.1, bf16[256,256]{1,0:T(8,128)(2,1)} %weight.1, bf16[128,128,128]{2,1,0:T(8,128)(2,1)} %local_tiles.1, ...), custom_call_target="tpu_custom_call" | custom-call | flops 12999999488 | bytes 25165824 | tf_op jit(solution)/shard_map/pallas_call | solution.py:312
  50.8 2.3 %copy.15 = bf16[2048,256]{1,0:T(8,128)(2,1)} copy(bf16[2048,256]{1,0:T(8,128)(2,1)} %shard_map.127) | data formatting | bytes 2097152
  (3 shorter events, 0.0 us)

commit v2 on v1

v2 whole, which is shorter than its diff:
```python
import functools

import jax
import jax.numpy as jnp
from jax import lax
from jax.experimental import pallas as pl
from jax.experimental.pallas import tpu as pltpu
from jax.sharding import PartitionSpec as P

MESH = pl.DeviceIdType.MESH
BF16 = jnp.bfloat16
F32 = jnp.float32
I32 = jnp.int32
I16 = jnp.int16
TILE = 128
PIECE = 64
OWN = 12


def offset(k):
    return 1 - k // 8, (2 + 3 * ((k // 2) % 4)) % 4, k % 2


def partner(r, k, sign):
    dy, dx, dc = offset(k)
    y, x, c = r // 8, (r // 2) % 4, r % 2
    return ((y + dy) % 2) * 8 + ((x + sign * dx + 4) % 4) * 2 + (c + dc) % 2


def dot(a, b):
    return jnp.dot(a, b, preferred_element_type=F32)


def slot_table(ids, live, bits, rows, cols, empty):
    slots = ids.shape[1]
    at_row = lax.broadcasted_iota(I32, (rows, slots), 0) == (ids >> bits)
    slot = lax.broadcasted_iota(I32, (rows, slots), 1) - empty
    value = jnp.where(jnp.logical_and(at_row, live > 0), slot, 0)
    col = ids & ((1 << bits) - 1)
    lane = lax.broadcasted_iota(I32, (rows, TILE), 1)
    table = jnp.zeros((rows, TILE), I32)
    for j in range(cols):
        least = jnp.min(jnp.where(col == j, value, 0), axis=1, keepdims=True)
        table = jnp.where(lane == j, least, table)
    return table + empty


def kernel(
    features,
    weight,
    local_tiles,
    local_ids,
    local_live,
    send_rows,
    send_count,
    edge_tiles,
    edge_ids,
    edge_live,
    hub_feats,
    hub_adj,
    hub_live,
    out,
    feats,
    wts,
    loc,
    edg,
    hraw,
    hubf,
    send,
    recv,
    acc,
    outv,
    rows_in,
    rowsk,
    colk,
    ids_e,
    live_e,
    ids_l,
    live_l,
    live_h,
    counts,
    tabv,
    tabs,
    in_sem,
    out_sem,
    ssem,
    rsem,
    hs_sem,
    hr_sem,
):
    r = lax.axis_index("row")
    l = lax.axis_index("loop")
    core = r % 2
    z, ylo = l // 2, l % 2
    sib = r + 1 - 2 * core
    nloc, nedge, nrow = local_tiles.shape[0], edge_tiles.shape[0], hub_adj.shape[0]

    def load(src, dst, n):
        return pltpu.make_async_copy(src, dst, in_sem.at[n])

    small = [
        load(src, dst, 6 + n)
        for n, (src, dst) in enumerate(
            [
                (send_rows, rows_in),
                (send_count, counts),
                (edge_ids, ids_e),
                (edge_live, live_e),
                (local_ids, ids_l),
                (local_live, live_l),
                (hub_live, live_h),
            ]
        )
    ]
    for c in small[:2]:
        c.start()
    def shard_half(half, owner):
        return pl.ds((half * 8 + owner) * TILE, TILE)

    c_feat = load(features, feats, 0)
    c_feat.start()
    c_hub = load(hub_feats.at[pl.ds(core * TILE, TILE)], hubf.at[shard_half(core, l)], 1)
    c_hub.start()
    for c in small[2:]:
        c.start()
    c_w = load(weight, wts, 2)
    c_w.start()
    c_loc = load(local_tiles, loc.at[pl.ds(0, nloc)], 3)
    c_loc.start()
    c_adj = load(hub_adj, hraw.at[pl.ds(0, nrow)], 4)
    c_adj.start()
    c_edge = load(edge_tiles, edg.at[pl.ds(0, nedge)], 5)
    c_edge.start()

    barrier = pltpu.get_barrier_semaphore()

    def greet(device):
        pl.semaphore_signal(barrier, inc=1, device_id=device, device_id_type=MESH)

    @pl.loop(0, 15)
    def _(n):
        greet({"row": (r + 1 + n) % 16, "loop": l})

    greet({"row": r, "loop": z * 2 + 1 - ylo})
    for dz in (1, 2, 3):
        greet({"row": r, "loop": ((z + dz) % 4) * 2 + ylo})

    for c in small[:2]:
        c.wait()
    rowsk[...] = jnp.full(rowsk.shape, -1, I32)
    slot = lax.broadcasted_iota(I32, (1, 4 * PIECE), 1)
    for k in range(16):
        s = partner(r, k, 1)
        row = rows_in[pl.ds(s, 1), :]
        rowsk[pl.ds(k, 1), :] = jnp.where(slot < counts[0, s], row, -1)
    colk[...] = jnp.transpose(rowsk[...])

    c_feat.wait()
    c_hub.wait()
    pl.semaphore_wait(barrier, 19)

    def remote(src, dst, s1, s2, device):
        return pltpu.make_async_remote_copy(
            src_ref=src, dst_ref=dst, send_sem=s1, recv_sem=s2, device_id=device, device_id_type=MESH
        )

    def piece(k, p, sign=1):
        return remote(
            send.at[k, pl.ds(p * PIECE, PIECE)],
            recv.at[p // 2, pl.ds(k * TILE + (p % 2) * PIECE, PIECE)],
            ssem.at[p, k],
            rsem.at[p, k],
            {"row": partner(r, k, 1), "loop": l},
        )

    def hub_step(n, lsrc, device):
        return remote(
            hubf.at[shard_half(core, lsrc)], hubf.at[shard_half(core, lsrc)], hs_sem.at[n], hr_sem.at[n], device
        )

    def hub_in(n, lsrc, half):
        at = hubf.at[shard_half(half, lsrc)]
        return remote(at, at, hs_sem.at[n], hr_sem.at[n], {"row": sib, "loop": l})

    l_y = z * 2 + 1 - ylo

    def zpeer(dz, own):
        return ((z + dz) % 4) * 2 + (ylo if own else 1 - ylo)

    hub_y = hub_step(0, l, {"row": r, "loop": l_y})
    hub_y.start()
    hub_z = [hub_step(dz, l, {"row": r, "loop": zpeer(dz, True)}) for dz in (1, 2, 3)]
    for c in hub_z:
        c.start()

    lane = lax.broadcasted_iota(I32, (4 * PIECE, TILE), 1).astype(I16)
    one, zero = jnp.ones(lane.shape, BF16), jnp.zeros(lane.shape, BF16)

    hub_f = [hub_step(3 + dz, l_y, {"row": r, "loop": zpeer(dz, True)}) for dz in (1, 2, 3)]

    def gather(p):
        cols = colk[pl.ds(pl.multiple_of(p * PIECE, PIECE), PIECE), :]
        for a in range(4):
            idx = jnp.concatenate(
                [jnp.broadcast_to(cols[:, k : k + 1], (PIECE, TILE)) for k in range(4 * a, 4 * a + 4)], 0
            )
            idx = idx.astype(I16)
            hot = [jnp.where(idx == lane + jnp.asarray(c * TILE, I16), one, zero) for c in range(feats.shape[0] // TILE)]
            picked = dot(jnp.concatenate(hot, 1), feats[...]).astype(BF16)
            for d in range(4):
                k = 4 * a + d
                part = picked[d * PIECE : (d + 1) * PIECE]
                if k == OWN:
                    recv[p // 2, pl.ds(pl.multiple_of(k * TILE + (p % 2) * PIECE, PIECE), PIECE), :] = part
                else:
                    send[k, pl.ds(pl.multiple_of(p * PIECE, PIECE), PIECE), :] = part
                    piece(k, p).start()

    @pl.loop(0, 2)
    def _(p):
        @pl.when(p == 1)
        def _():
            hub_in(0, l_y, core).wait_recv()
            for c in hub_f:
                c.start()

        gather(p)

    loc[nloc] = jnp.zeros((TILE, TILE), BF16)
    edg[nedge] = jnp.zeros((TILE, TILE), BF16)
    hraw[nrow] = jnp.zeros((TILE, hraw.shape[2]), BF16)
    for c in small[2:]:
        c.wait()
    tabv[0:16, :] = slot_table(ids_e[...][None, :], live_e[...][None, :], 5, 16, 32, nedge)
    tabv[16:32, :] = slot_table(ids_l[...], live_l[...], 4, 16, 16, nloc)
    cell_row = lax.broadcasted_iota(I32, live_h.shape, 0)
    tabv[32:48, 0:16] = jnp.where(live_h[...] == 0, nrow, cell_row)
    c_tab = load(tabv, tabs, 13)
    c_tab.start()

    def blocks(n):
        step = acc.shape[0] // n

        def over(body):
            @pl.loop(0, n)
            def _(m):
                body(m, pl.ds(pl.multiple_of(m * step, step), step))

        return over

    def laid(i0, n, cells):
        lines = [jnp.concatenate([cell(i0 + i) for cell in cells], 1) for i in range(n)]
        return jnp.concatenate(lines, 0)

    def local_cell(j):
        return lambda i: loc[tabs[16 + i, j]]

    def hub_cell(b):
        return lambda i: hraw[tabs[32 + i, b], :, b * TILE : (b + 1) * TILE]

    def edge_cell(k, h):
        col = 2 * partner(r, k, -1) + h
        return lambda i: edg[tabs[i, col]]

    c_tab.wait()
    c_loc.wait()
    cells = [local_cell(j) for j in range(16)]

    @blocks(4)
    def _(m, at):
        acc[at, :] = dot(laid(4 * m, 4, cells), feats[...])

    for dz in (1, 2, 3):
        hub_in(dz, ((z + 4 - dz) % 4) * 2 + ylo, core).wait_recv()
        hub_in(3 + dz, ((z + 4 - dz) % 4) * 2 + 1 - ylo, core).wait_recv()
    mine, other = pl.ds(core * 8 * TILE, 8 * TILE), pl.ds((1 - core) * 8 * TILE, 8 * TILE)
    hub_c = remote(hubf.at[mine], hubf.at[mine], hs_sem.at[7], hr_sem.at[7], {"row": sib, "loop": l})
    hub_c.start()

    @pl.loop(2, 4)
    def _(p):
        gather(p)

    c_edge.wait()
    for p in (0, 1):
        for k in range(16):
            if k != OWN:
                piece(k, p).wait_recv()
    cells = [edge_cell(k, 0) for k in range(16)]

    @blocks(4)
    def _(m, at):
        acc[at, :] += dot(laid(4 * m, 4, cells), recv[0])

    c_adj.wait()
    remote(hubf.at[other], hubf.at[other], hs_sem.at[7], hr_sem.at[7], {"row": sib, "loop": l}).wait_recv()
    cells = [hub_cell(b) for b in list(range(0, 16, 2)) + list(range(1, 16, 2))]

    @blocks(4)
    def _(m, at):
        acc[at, :] += dot(laid(4 * m, 4, cells), hubf[...])

    group = 4
    for g in range(4):
        span = slice(g * group * TILE, (g + 1) * group * TILE)
        for p in (2, 3):
            for k in range(g * group, (g + 1) * group):
                if k != OWN:
                    piece(k, p).wait_recv()
        cells = [edge_cell(k, 1) for k in range(g * group, (g + 1) * group)]
        if g < 3:

            @blocks(2)
            def _(m, at):
                acc[at, :] += dot(laid(8 * m, 8, cells), recv[1, span, :])

    c_w.wait()

    @blocks(4)
    def _(m, at):
        agg = (acc[at, :] + dot(laid(4 * m, 4, cells), recv[1, span, :])).astype(BF16)
        outv[at, :] = jnp.maximum(dot(agg, wts[...]), 0.0).astype(BF16)
        pltpu.make_async_copy(outv.at[at], out.at[at], out_sem.at[m]).start()

    hub_y.wait_send()
    for c in hub_z + hub_f:
        c.wait_send()
    hub_c.wait_send()

    @pl.loop(0, 4)
    def _(p):
        for k in range(16):
            if k != OWN:
                piece(k, p).wait_send()

    @blocks(4)
    def _(m, at):
        pltpu.make_async_copy(outv.at[at], out.at[at], out_sem.at[m]).wait()


def per_device(
    features,
    weight,
    local_tiles,
    local_ids,
    local_live,
    send_rows,
    send_count,
    edge_tiles,
    edge_ids,
    edge_live,
    hub_feats,
    hub_adj,
    hub_live,
):
    rows, width = features.shape
    nloc, nedge = local_tiles.shape[0], edge_tiles.shape[0]
    hbm = pl.BlockSpec(memory_space=pl.ANY)
    dma = pltpu.SemaphoreType.DMA
    return pl.pallas_call(
        kernel,
        out_shape=jax.ShapeDtypeStruct((rows, width), BF16),
        in_specs=[hbm] * 13,
        out_specs=hbm,
        scratch_shapes=[
            pltpu.VMEM((rows, width), BF16),
            pltpu.VMEM((width, width), BF16),
            pltpu.VMEM((nloc + 1, TILE, TILE), BF16),
            pltpu.VMEM((nedge + 1, TILE, TILE), BF16),
            pltpu.VMEM((rows // TILE + 1, TILE, 16 * TILE), BF16),
            pltpu.VMEM((16 * TILE, width), BF16),
            pltpu.VMEM((16, 4 * PIECE, width), BF16),
            pltpu.VMEM((2, 16 * TILE, width), BF16),
            pltpu.VMEM((rows, width), F32),
            pltpu.VMEM((rows, width), BF16),
            pltpu.VMEM((16, 4 * PIECE), I32),
            pltpu.VMEM((TILE, 4 * PIECE), I32),
            pltpu.VMEM((4 * PIECE, TILE), I32),
            pltpu.VMEM((nedge,), I32),
            pltpu.VMEM((nedge,), I32),
            pltpu.VMEM((1, nloc), I32),
            pltpu.VMEM((1, nloc), I32),
            pltpu.VMEM(hub_live.shape, I32),
            pltpu.SMEM(send_count.shape, I32),
            pltpu.VMEM((48, TILE), I32),
            pltpu.SMEM((48, TILE), I32),
            dma((14,)),
            dma((4,)),
            dma((4, 16)),
            dma((4, 16)),
            dma((8,)),
            dma((8,)),
        ],
        compiler_params=pltpu.CompilerParams(
            collective_id=0, has_side_effects=True, vmem_limit_bytes=60 * 1024 * 1024
        ),
        cost_estimate=pl.CostEstimate(flops=13 * 10**9, bytes_accessed=24 * 2**20, transcendentals=0),
    )(
        features,
        weight,
        local_tiles,
        local_ids[None, :],
        local_live[None, :],
        send_rows[0],
        send_count,
        edge_tiles,
        edge_ids,
        edge_live,
        hub_feats,
        hub_adj.reshape(rows // TILE, TILE, hub_adj.shape[1]),
        hub_live,
    )


def solution(mesh):
    both = ("row", "loop")
    placed = (
        P(both, None),
        P(),
        P(both, None, None),
        P(both),
        P(both),
        P(both, None, None),
        P(both, None),
        P(both, None, None),
        P(both),
        P(both),
        P("loop", None),
        P(both, None),
        P(both, None),
    )
    return jax.shard_map(per_device, mesh=mesh, in_specs=placed, out_specs=P(both, None), check_vma=False)
```

time: 53.4 us -> 43.7 us (0.82)
  Pallas kernels: 46.8 us -> 41.2 us
  other arithmetic: 3.9 us -> 0 us
    pallas_call x1, Pallas kernels: 46.8 us -> 41.2 us  [per_device(): pl.pallas_call(kernel, out_shape=jax.ShapeDtypeStruct((rows, width), BF16...]
    concatenate x2 -> x0, other arithmetic: 1.36 us -> none  [the longest x1 0.76 us: slot_table(): ids = jnp.concatenate([edge_ids, local_ids + 512])]
    gt x1 -> x0, other arithmetic: 0.78 us -> none  [slot_table(): live = jnp.concatenate([edge_live, local_live]) > 0]
    select_n x1 -> x0, other arithmetic: 0.7 us -> none  [slot_table(): hub = jnp.where(hub_live == 0, nrow, jnp.arange(nrow)[:, None])]
    add x2 -> x0, other arithmetic: 0.66 us -> none  [the longest x1 0.66 us: slot_table(): ids = jnp.concatenate([edge_ids, local_ids + 512])]
where the time goes in v2:
time: 43.7 us; the launch traced here: 43.5 us
  Pallas kernels  41.2 us (94%)
  local copies, waits for them, and re-layouts  2.26 us (5%)
    pallas_call x1, Pallas kernels, per_device(): pl.pallas_call(kernel, out_shape=jax.ShapeDtypeStruct((rows, width), BF16...  41.2 us
    unnamed x1, local copies, waits for them, and re-layouts  2.26 us

profile of v2, /device:TPU:1, one launch (start us, length us, event | category | flops | bytes accessed | tf_op | source)
XLA Modules:
  0.0 43.5 jit_solution(8293824079752817329)
XLA Ops:
  0.0 41.2 %shard_map.127 = bf16[2048,256]{1,0:T(8,128)(2,1)} custom-call(bf16[2048,256]{1,0:T(8,128)(2,1)} %features.1, bf16[256,256]{1,0:T(8,128)(2,1)} %weight.1, bf16[128,128,128]{2,1,0:T(8,128)(2,1)} %local_tiles.1, s32[1,128]{1,0:T(1,128)} %bitcast.6, s32[1,128]{1,0:T(1,128)} %bitcast.7, s32[16,256]{1,0:T(8,128)} %bitcast.5, s32[1,16]{1,0:T(1,128)} %send_count.1, ...), custom_call_target="tpu_custom_call" | custom-call | flops 12999999488 | bytes 25165824 | tf_op jit(solution)/shard_map/pallas_call | solution.py:360
  41.3 2.3 %copy.15 = bf16[2048,256]{1,0:T(8,128)(2,1)} copy(bf16[2048,256]{1,0:T(8,128)(2,1)} %shard_map.127) | data formatting | bytes 2097152

commit v3 on v2

--- a/solution.py
+++ b/solution.py
@@ -14,11 +14,12 @@
 I16 = jnp.int16
 TILE = 128
 PIECE = 64
-OWN = 12
+OWN = 6
 
 
 def offset(k):
-    return 1 - k // 8, (2 + 3 * ((k // 2) % 4)) % 4, k % 2
+    dc, b, j = k // 8, (k // 4) % 2, k % 4
+    return (1 + j + b) % 2, (2 + 3 * j) % 4, dc
 
 
 def partner(r, k, sign):
@@ -47,7 +48,6 @@
 
 def kernel(
     features,
-    weight,
     local_tiles,
     local_ids,
     local_live,
@@ -61,7 +61,6 @@
     hub_live,
     out,
     feats,
-    wts,
     loc,
     edg,
     hraw,
@@ -123,8 +122,6 @@
     c_hub.start()
     for c in small[2:]:
         c.start()
-    c_w = load(weight, wts, 2)
-    c_w.start()
     c_loc = load(local_tiles, loc.at[pl.ds(0, nloc)], 3)
     c_loc.start()
     c_adj = load(hub_adj, hraw.at[pl.ds(0, nrow)], 4)
@@ -198,23 +195,22 @@
 
     hub_f = [hub_step(3 + dz, l_y, {"row": r, "loop": zpeer(dz, True)}) for dz in (1, 2, 3)]
 
-    def gather(p):
+    def gather(p, a):
         cols = colk[pl.ds(pl.multiple_of(p * PIECE, PIECE), PIECE), :]
-        for a in range(4):
-            idx = jnp.concatenate(
-                [jnp.broadcast_to(cols[:, k : k + 1], (PIECE, TILE)) for k in range(4 * a, 4 * a + 4)], 0
-            )
-            idx = idx.astype(I16)
-            hot = [jnp.where(idx == lane + jnp.asarray(c * TILE, I16), one, zero) for c in range(feats.shape[0] // TILE)]
-            picked = dot(jnp.concatenate(hot, 1), feats[...]).astype(BF16)
-            for d in range(4):
-                k = 4 * a + d
-                part = picked[d * PIECE : (d + 1) * PIECE]
-                if k == OWN:
-                    recv[p // 2, pl.ds(pl.multiple_of(k * TILE + (p % 2) * PIECE, PIECE), PIECE), :] = part
-                else:
-                    send[k, pl.ds(pl.multiple_of(p * PIECE, PIECE), PIECE), :] = part
-                    piece(k, p).start()
+        idx = jnp.concatenate(
+            [jnp.broadcast_to(cols[:, k : k + 1], (PIECE, TILE)) for k in range(4 * a, 4 * a + 4)], 0
+        )
+        idx = idx.astype(I16)
+        hot = [jnp.where(idx == lane + jnp.asarray(c * TILE, I16), one, zero) for c in range(feats.shape[0] // TILE)]
+        picked = dot(jnp.concatenate(hot, 1), feats[...]).astype(BF16)
+        for d in range(4):
+            k = 4 * a + d
+            part = picked[d * PIECE : (d + 1) * PIECE]
+            if k == OWN:
+                recv[p // 2, pl.ds(pl.multiple_of(k * TILE + (p % 2) * PIECE, PIECE), PIECE), :] = part
+            else:
+                send[k, pl.ds(pl.multiple_of(p * PIECE, PIECE), PIECE), :] = part
+                piece(k, p).start()
 
     @pl.loop(0, 2)
     def _(p):
@@ -224,7 +220,8 @@
             for c in hub_f:
                 c.start()
 
-        gather(p)
+        for a in range(4):
+            gather(p, a)
 
     loc[nloc] = jnp.zeros((TILE, TILE), BF16)
     edg[nedge] = jnp.zeros((TILE, TILE), BF16)
@@ -277,9 +274,11 @@
     hub_c = remote(hubf.at[mine], hubf.at[mine], hs_sem.at[7], hr_sem.at[7], {"row": sib, "loop": l})
     hub_c.start()
 
-    @pl.loop(2, 4)
-    def _(p):
-        gather(p)
+    for a in range(4):
+
+        @pl.loop(2, 4)
+        def _(p):
+            gather(p, a)
 
     c_edge.wait()
     for p in (0, 1):
@@ -300,26 +299,30 @@
     def _(m, at):
         acc[at, :] += dot(laid(4 * m, 4, cells), hubf[...])
 
-    group = 4
-    for g in range(4):
-        span = slice(g * group * TILE, (g + 1) * group * TILE)
-        for p in (2, 3):
-            for k in range(g * group, (g + 1) * group):
-                if k != OWN:
+    def edge_group(first, last):
+        for k in range(first, last):
+            if k != OWN:
+                for p in (2, 3):
                     piece(k, p).wait_recv()
-        cells = [edge_cell(k, 1) for k in range(g * group, (g + 1) * group)]
-        if g < 3:
-
-            @blocks(2)
-            def _(m, at):
-                acc[at, :] += dot(laid(8 * m, 8, cells), recv[1, span, :])
-
-    c_w.wait()
-
-    @blocks(4)
-    def _(m, at):
-        agg = (acc[at, :] + dot(laid(4 * m, 4, cells), recv[1, span, :])).astype(BF16)
-        outv[at, :] = jnp.maximum(dot(agg, wts[...]), 0.0).astype(BF16)
+        return slice(first * TILE, last * TILE), [edge_cell(k, 1) for k in range(first, last)]
+
+    span, cells = edge_group(0, 8)
+
+    @blocks(4)
+    def _(m, at):
+        acc[at, :] += dot(laid(4 * m, 4, cells), recv[1, span, :])
+
+    span2, cells2 = edge_group(8, 12)
+
+    @blocks(2)
+    def _(m, at):
+        acc[at, :] += dot(laid(8 * m, 8, cells2), recv[1, span2, :])
+
+    span3, cells3 = edge_group(12, 16)
+
+    @blocks(4)
+    def _(m, at):
+        outv[at, :] = (acc[at, :] + dot(laid(4 * m, 4, cells3), recv[1, span3, :])).astype(BF16)
         pltpu.make_async_copy(outv.at[at], out.at[at], out_sem.at[m]).start()
 
     hub_y.wait_send()
@@ -357,14 +360,13 @@
     nloc, nedge = local_tiles.shape[0], edge_tiles.shape[0]
     hbm = pl.BlockSpec(memory_space=pl.ANY)
     dma = pltpu.SemaphoreType.DMA
-    return pl.pallas_call(
+    agg = pl.pallas_call(
         kernel,
         out_shape=jax.ShapeDtypeStruct((rows, width), BF16),
-        in_specs=[hbm] * 13,
+        in_specs=[hbm] * 12,
         out_specs=hbm,
         scratch_shapes=[
             pltpu.VMEM((rows, width), BF16),
-            pltpu.VMEM((width, width), BF16),
             pltpu.VMEM((nloc + 1, TILE, TILE), BF16),
             pltpu.VMEM((nedge + 1, TILE, TILE), BF16),
             pltpu.VMEM((rows // TILE + 1, TILE, 16 * TILE), BF16),
@@ -397,7 +399,6 @@
         cost_estimate=pl.CostEstimate(flops=13 * 10**9, bytes_accessed=24 * 2**20, transcendentals=0),
     )(
         features,
-        weight,
         local_tiles,
         local_ids[None, :],
         local_live[None, :],
@@ -410,6 +411,7 @@
         hub_adj.reshape(rows // TILE, TILE, hub_adj.shape[1]),
         hub_live,
     )
+    return jnp.maximum(dot(agg, weight), 0.0).astype(BF16)
 
 
 def solution(mesh):

time: 43.7 us -> 40.3 us (0.922)
  Pallas kernels: 41.2 us -> 37.5 us
  matrix products: 0 us -> 2.64 us
  local copies, waits for them, and re-layouts: 2.26 us -> 0.01 us
    pallas_call x1, Pallas kernels: 41.2 us -> 37.5 us  [per_device(): pl.pallas_call(kernel, out_shape=jax.ShapeDtypeStruct((rows, width), BF16...]
    dot_general x0 -> x1, matrix products: none -> 2.64 us  [dot(): return jnp.dot(a, b, preferred_element_type=F32)]
    unnamed x1 -> x2, local copies, waits for them, and re-layouts: 2.26 us -> 0.01 us
where the time goes in v3:
time: 40.3 us; the launch traced here: 40.2 us
  Pallas kernels  37.5 us (93%)
  matrix products  2.64 us (7%)
    pallas_call x1, Pallas kernels, per_device(): pl.pallas_call(kernel, out_shape=jax.ShapeDtypeStruct((rows, width), BF16...  37.5 us
    dot_general x1, matrix products, dot(): return jnp.dot(a, b, preferred_element_type=F32)  2.64 us

profile of v3, /device:TPU:1, one launch (start us, length us, event | category | flops | bytes accessed | tf_op | source)
XLA Modules:
  0.0 40.2 jit_solution(15721062398383137748)
XLA Ops:
  0.0 0.0 copy-start
  0.0 37.5 %shard_map.127 = bf16[2048,256]{1,0:T(8,128)(2,1)} custom-call(bf16[2048,256]{1,0:T(8,128)(2,1)} %features.1, bf16[128,128,128]{2,1,0:T(8,128)(2,1)} %local_tiles.1, s32[1,128]{1,0:T(1,128)} %bitcast.8, s32[1,128]{1,0:T(1,128)} %bitcast.9, s32[16,256]{1,0:T(8,128)} %bitcast.7, s32[1,16]{1,0:T(1,128)} %send_count.1, bf16[288,128,128]{2,1,0:T(8,128)(2,1)} %edge_tiles.1, ...), custom_call_target="tpu_custom_call" | custom-call | flops 12999999488 | bytes 25165824 | tf_op jit(solution)/shard_map/pallas_call | solution.py:363
  37.6 0.0 copy-done
  37.6 2.6 %fusion = bf16[2048,256]{1,0:T(8,128)(2,1)} fusion(bf16[2048,256]{1,0:T(8,128)(2,1)} %shard_map.127, bf16[256,256]{1,0:T(8,128)(2,1)S(1)} %copy-done), kind=kOutput, calls=%fused_computation.1 | convolution fusion | flops 269484032 | bytes 2228224 | tf_op jit(solution)/shard_map/dot_general | solution.py:32
Async XLA Ops:
  0.0 37.6 %copy-start = (bf16[256,256]{1,0:T(8,128)(2,1)S(1)}, bf16[256,256]{1,0:T(8,128)(2,1)}, u32[]{:S(2)}) copy-start(bf16[256,256]{1,0:T(8,128)(2,1)} %param.14) | copy-start | bytes 393220

commit v4 on v3

--- a/solution.py
+++ b/solution.py
@@ -68,7 +68,6 @@
     send,
     recv,
     acc,
-    outv,
     rows_in,
     rowsk,
     colk,
@@ -81,7 +80,6 @@
     tabv,
     tabs,
     in_sem,
-    out_sem,
     ssem,
     rsem,
     hs_sem,
@@ -322,8 +320,8 @@
 
     @blocks(4)
     def _(m, at):
-        outv[at, :] = (acc[at, :] + dot(laid(4 * m, 4, cells3), recv[1, span3, :])).astype(BF16)
-        pltpu.make_async_copy(outv.at[at], out.at[at], out_sem.at[m]).start()
+        out[at, :] = (acc[at, :] + dot(laid(4 * m, 4, cells3), recv[1, span3, :])).astype(BF16)
+
 
     hub_y.wait_send()
     for c in hub_z + hub_f:
@@ -335,10 +333,6 @@
         for k in range(16):
             if k != OWN:
                 piece(k, p).wait_send()
-
-    @blocks(4)
-    def _(m, at):
-        pltpu.make_async_copy(outv.at[at], out.at[at], out_sem.at[m]).wait()
 
 
 def per_device(
@@ -358,13 +352,13 @@
 ):
     rows, width = features.shape
     nloc, nedge = local_tiles.shape[0], edge_tiles.shape[0]
-    hbm = pl.BlockSpec(memory_space=pl.ANY)
+    hbm = pl.BlockSpec(memory_space=pltpu.HBM)
     dma = pltpu.SemaphoreType.DMA
     agg = pl.pallas_call(
         kernel,
         out_shape=jax.ShapeDtypeStruct((rows, width), BF16),
         in_specs=[hbm] * 12,
-        out_specs=hbm,
+        out_specs=pl.BlockSpec(memory_space=pltpu.VMEM),
         scratch_shapes=[
             pltpu.VMEM((rows, width), BF16),
             pltpu.VMEM((nloc + 1, TILE, TILE), BF16),
@@ -374,7 +368,6 @@
             pltpu.VMEM((16, 4 * PIECE, width), BF16),
             pltpu.VMEM((2, 16 * TILE, width), BF16),
             pltpu.VMEM((rows, width), F32),
-            pltpu.VMEM((rows, width), BF16),
             pltpu.VMEM((16, 4 * PIECE), I32),
             pltpu.VMEM((TILE, 4 * PIECE), I32),
             pltpu.VMEM((4 * PIECE, TILE), I32),
@@ -387,17 +380,16 @@
             pltpu.VMEM((48, TILE), I32),
             pltpu.SMEM((48, TILE), I32),
             dma((14,)),
-            dma((4,)),
             dma((4, 16)),
             dma((4, 16)),
             dma((8,)),
             dma((8,)),
         ],
         compiler_params=pltpu.CompilerParams(
-            collective_id=0, has_side_effects=True, vmem_limit_bytes=60 * 1024 * 1024
+            collective_id=0, has_side_effects=True, vmem_limit_bytes=40 * 1024 * 1024
         ),
         cost_estimate=pl.CostEstimate(flops=13 * 10**9, bytes_accessed=24 * 2**20, transcendentals=0),
-    )(
+    )(*[pltpu.with_memory_space_constraint(v, pltpu.HBM) for v in (
         features,
         local_tiles,
         local_ids[None, :],
@@ -410,7 +402,7 @@
         hub_feats,
         hub_adj.reshape(rows // TILE, TILE, hub_adj.shape[1]),
         hub_live,
-    )
+    )])
     return jnp.maximum(dot(agg, weight), 0.0).astype(BF16)
 
 

time: 40.3 us -> 38.4 us (0.953)
  matrix products: 2.64 us -> 1.41 us
  Pallas kernels: 37.5 us -> 36.9 us
    dot_general x1, matrix products: 2.64 us -> 1.41 us  [dot(): return jnp.dot(a, b, preferred_element_type=F32)]
    pallas_call x1, Pallas kernels: 37.5 us -> 36.9 us  [per_device(): pl.pallas_call(kernel, out_shape=jax.ShapeDtypeStruct((rows, width), BF16...]
where the time goes in v4:
time: 38.4 us; the launch traced here: 38.3 us
  Pallas kernels  36.9 us (96%)
  matrix products  1.41 us (4%)
    pallas_call x1, Pallas kernels, per_device(): pl.pallas_call(kernel, out_shape=jax.ShapeDtypeStruct((rows, width), BF16...  36.9 us
    dot_general x1, matrix products, dot(): return jnp.dot(a, b, preferred_element_type=F32)  1.41 us

profile of v4, /device:TPU:1, one launch (start us, length us, event | category | flops | bytes accessed | tf_op | source)
XLA Modules:
  0.0 38.3 jit_solution(269647608566879638)
XLA Ops:
  0.0 0.0 copy-start
  0.0 36.9 %shard_map.127 = bf16[2048,256]{1,0:T(8,128)(2,1)S(1)} custom-call(bf16[2048,256]{1,0:T(8,128)(2,1)} %features.1, bf16[128,128,128]{2,1,0:T(8,128)(2,1)} %local_tiles.1, s32[1,128]{1,0:T(1,128)} %bitcast.8, s32[1,128]{1,0:T(1,128)} %bitcast.9, s32[16,256]{1,0:T(8,128)} %bitcast.7, s32[1,16]{1,0:T(1,128)} %send_count.1, bf16[288,128,128]{2,1,0:T(8,128)(2,1)} %edge_tiles.1, ...), custom_call_target="tpu_custom_call" | custom-call | flops 12999999488 | bytes 25165824 | tf_op jit(solution)/shard_map/pallas_call | solution.py:357
  36.9 0.0 copy-done
  36.9 1.4 %fusion = bf16[2048,256]{1,0:T(8,128)(2,1)} fusion(bf16[2048,256]{1,0:T(8,128)(2,1)S(1)} %shard_map.127, bf16[256,256]{1,0:T(8,128)(2,1)S(1)} %copy-done), kind=kOutput, calls=%fused_computation.1 | convolution fusion | flops 269484032 | bytes 2228224 | tf_op jit(solution)/shard_map/dot_general | solution.py:32
Async XLA Ops:
  0.0 36.9 %copy-start = (bf16[256,256]{1,0:T(8,128)(2,1)S(1)}, bf16[256,256]{1,0:T(8,128)(2,1)}, u32[]{:S(2)}) copy-start(bf16[256,256]{1,0:T(8,128)(2,1)} %param.14) | copy-start | bytes 393220
